TPU v7x, 32 devices: a whole 2x2x4 slice. The times are simulated.
32 devices in a mesh: wide: 16 (over z, y, x), clus: 2 (over core).
Axes of the slice: x: 2, y: 2, z: 4, core: 2. Of those that a mesh axis runs over, the one named last changes fastest.
Arguments:
- duals: bfloat16 [96, 64, 3840], P(None, ('wide', 'clus')), may hold values from -6 to 6
- kernel: bfloat16 [64, 6, 3840], P(('wide', 'clus')), may hold values from -0.29882812 to 0.29882812
- sub_counts: int32 [32], P(('wide', 'clus')), may hold values from 1 to 2, as said below
- dual_sizes: int32 [64], P(('wide', 'clus')), may hold values from 1920 to 3840, as said below
- cluster_factor: float32 [16, 24, 24], P('wide'), as said below
- coarse_map: int32 [16, 24], P('wide'), may hold values from 0 to 383, as said below
- coarse_inverse: float32 [384, 384], P(None, 'clus'), as said below
Outputs:
- projected: bfloat16 [96, 64, 3840], P(None, ('wide', 'clus'))
Inputs may be any that keep to these rules, and one draw needn't show every extreme that they name: `sub_counts`: each device holds 1 to 2 subdomains; some device holds 2. `dual_sizes`: some slot has the full 3840. `coarse_map`: the rows of cluster w map into the 48 global rows that begin at w * 24, counted modulo 384. `cluster_factor`: lower triangular with diagonal entries between 1 and 2. `coarse_inverse`: diagonal entries between 1 and 2.
All inputs are finite; a program needn't handle non-finite values.
Results may differ from a plain program's by a relative error of at most 0.0018.
Values sent between devices are 32-bit elements; how exact they have to be, the bound alone decides.
No kernel may reach another device: no remote copies, remote signals or barrier semaphores. Data moves between devices by JAX's collectives and lax.ppermute only.
A program may use at most 64 MiB of HBM per device.

v0:
```python
import jax
import jax.numpy as jnp
from jax import lax
from jax.sharding import PartitionSpec as P


def per_device(duals, kernel, sub_counts, dual_sizes, cluster_factor, coarse_map, coarse_inverse):
    rhs_count, sub_count, dual_width = duals.shape
    mode_count = kernel.shape[1]
    hi = lax.Precision.HIGHEST
    position = lax.broadcasted_iota(jnp.int32, (sub_count, dual_width), 1)
    slot_index = lax.broadcasted_iota(jnp.int32, (sub_count, dual_width), 0)
    active = (position < dual_sizes[:, None]) & (slot_index < sub_counts[0])
    masked = jnp.where(active[:, None, :], kernel, jnp.zeros_like(kernel))
    local = jnp.einsum("rsi,ski->rsk", duals, masked, preferred_element_type=jnp.float32)
    local = local.reshape(rhs_count, sub_count * mode_count)
    cluster_vec = lax.all_gather(local, "clus", axis=1, tiled=True)
    lower = cluster_factor[0]
    rows_map = coarse_map[0]
    cluster_rows = rows_map.shape[0]
    global_rows = coarse_inverse.shape[0]
    forward = lax.linalg.triangular_solve(lower, cluster_vec.T, left_side=True, lower=True).T
    one_hot = (
        rows_map[:, None] == lax.broadcasted_iota(jnp.int32, (cluster_rows, global_rows), 1)
    ).astype(jnp.float32)
    part_sum = jnp.dot(forward, one_hot, precision=hi)
    gsum = lax.psum(part_sum, "wide")
    beta_part = jnp.dot(gsum, coarse_inverse, precision=hi)
    beta = lax.all_gather(beta_part, "clus", axis=1, tiled=True)
    back = jnp.dot(beta, one_hot.T, precision=hi)
    corr = lax.linalg.triangular_solve(
        lower, (forward - back).T, left_side=True, lower=True, transpose_a=True
    )
    own_rows = lax.dynamic_slice_in_dim(
        corr, lax.axis_index("clus") * sub_count * mode_count, sub_count * mode_count, 0
    )
    own_corr = own_rows.T.reshape(rhs_count, sub_count, mode_count).astype(jnp.bfloat16)
    delta = jnp.einsum("rsk,ski->rsi", own_corr, masked, preferred_element_type=jnp.float32)
    return (duals.astype(jnp.float32) - delta).astype(jnp.bfloat16)


def solution(mesh):
    in_specs = (
        P(None, ("wide", "clus"), None),
        P(("wide", "clus"), None, None),
        P(("wide", "clus")),
        P(("wide", "clus")),
        P("wide", None, None),
        P("wide", None),
        P(None, "clus"),
    )
    out_specs = P(None, ("wide", "clus"), None)
    return jax.shard_map(
        per_device, mesh=mesh, in_specs=in_specs, out_specs=out_specs, check_vma=False
    )
```

profile of v0, /device:TPU:0, one launch (start us, length us, event | category | flops | bytes accessed | tf_op | source)
XLA Modules:
  0.0 140.0 jit_solution(6165059862386261918)
XLA Ops:
  6.5 0.0 copy-start
  6.5 0.0 copy-start.2
  6.5 0.0 all-reduce.2.cloned.1.call-start
  7.3 0.7 fusion.16
  8.0 1.8 %custom-call.5 = f32[1,24,24]{1,2,0:T(8,128)S(1)} custom-call(f32[1,24,24]{2,1,0:T(8,128)S(1)} %fusion.16), custom_call_target="InvertDiagBlocksLowerTriangular" | custom-call | tf_op jit(solution)/shard_map/triangular_solve | solution.py:31
  9.8 0.8 compare_and_fusion
  10.6 1.0 broadcast_select_fusion
  11.6 0.0 copy-start.1
  11.6 2.0 %fusion.4 = f32[96,2,6]{0,2,1:T(8,128)S(1)} fusion(bf16[96,2,3840]{2,1,0:T(2,128)(2,1)} %param.7, bf16[2,6,3840]{2,0,1:T(2,128)(2,1)S(1)} %broadcast_select_fusion), kind=kOutput, calls=%fused_computation.6 | convolution fusion | flops 8847360 | bytes 1571328 | tf_op jit(solution)/shard_map/rsi,ski->rsk/dot_general | solution.py:15
  13.5 2.0 %all-gather = f32[2,12,96]{2,1,0:T(8,128)S(1)} all-gather(f32[1,12,96]{2,1,0:T(8,128)S(1)} %bitcast.34), channel_id=1, replica_groups=mesh['wide'=16,'clus'=2] {'clus'}, dimensions={0}, use_global_device_ids=true | all-gather | bytes 13824 | tf_op jit(solution)/shard_map/all_gather | solution.py:17
  15.5 0.2 fusion.14
  15.7 0.0 copy-done.2
  15.7 0.9 fusion.9
  16.7 0.0 all-reduce.2.cloned.1.call-update
  16.7 109.5 %all-reduce.2.cloned.1.call-done = f32[96,384]{1,0:T(8,128)} async-done(((f32[96,384]{1,0:T(8,128)}), f32[96,384]{1,0:T(8,128)}) %all-reduce.2.cloned.1.call-update) | async-done | bytes 147472 | tf_op jit(solution)/shard_map/psum | solution.py:27
  126.2 0.0 copy-done
  126.2 1.3 fusion.18
  127.5 1.9 %all_gather.7 = f32[96,384]{0,1:T(8,128)S(1)} all-gather(f32[96,192]{0,1:T(8,128)S(1)} %fusion.18), channel_id=1, replica_groups=mesh['wide'=16,'clus'=2] {'clus'}, dimensions={1}, use_global_device_ids=true | all-gather | bytes 221184 | tf_op jit(solution)/shard_map/all_gather | solution.py:29
  129.5 0.2 convolution_subtract_fusion
  129.7 0.1 fusion.12
  129.9 0.0 copy-done.1
  129.9 0.6 fusion.1
  130.5 2.6 %copy.23 = bf16[96,2,3840]{2,1,0:T(2,128)(2,1)} copy(bf16[96,2,3840]{2,0,1:T(8,128)(2,1)S(1)} %fusion.1) | data formatting | bytes 2949120 | tf_op jit(solution)/shard_map/convert_element_type | solution.py:39
  (5 shorter events, 0.1 us)
Async XLA Ops:
  6.5 119.7 %copy-start = (f32[384,192]{0,1:T(8,128)S(1)}, f32[384,192]{0,1:T(8,128)}, u32[]{:S(2)}) copy-start(f32[384,192]{0,1:T(8,128)} %param.13) | copy-start | bytes 884740
  6.5 9.2 %copy-start.2 = (s32[1,24]{1,0:T(1,128)S(1)}, s32[1,24]{1,0:T(1,128)}, u32[]{:S(2)}) copy-start(s32[1,24]{1,0:T(1,128)} %param.12) | copy-start | bytes 292
  6.5 119.7 %all-reduce.2.cloned.1.call-start = ((), (), s32[]{:S(2)}) async-start(), calls=%async_computation | async-start | bytes 294912 | tf_op jit(solution)/shard_map/psum | solution.py:27
  11.6 118.3 %copy-start.1 = (bf16[96,2,3840]{2,1,0:T(2,128)(2,1)S(1)}, bf16[96,2,3840]{2,1,0:T(2,128)(2,1)}, u32[]{:S(2)}) copy-start(bf16[96,2,3840]{2,1,0:T(2,128)(2,1)} %param.7) | copy-start | bytes 4423684
Sparse Core Ops, SparseCore 0:
  16.8 109.3 all-reduce.1
where the time goes:
time: 140 us
  waiting for transfers between devices  110 us (79%)
  between operations  14.2 us (10%)
  matrix products  5.34 us (4%)
  other arithmetic  4.31 us (3%)
  blocking collectives  3.92 us (3%)
  local copies, waits for them, and re-layouts  2.7 us (2%)
    psum x1, waiting for transfers between devices, per_device(): gsum = lax.psum(part_sum, 'wide')  110 us
  transfers between devices with their start and end apart: 1, of which 1 were waited for; matrix products, arithmetic and copies ran while one was open for 0% of the time, Pallas kernels for 0%

commit v1 on v0

--- a/solution.py
+++ b/solution.py
@@ -24,7 +24,8 @@
         rows_map[:, None] == lax.broadcasted_iota(jnp.int32, (cluster_rows, global_rows), 1)
     ).astype(jnp.float32)
     part_sum = jnp.dot(forward, one_hot, precision=hi)
-    gsum = lax.psum(part_sum, "wide")
+    terms = lax.all_gather(part_sum, "wide", axis=0, tiled=False)
+    gsum = terms.sum(axis=0)
     beta_part = jnp.dot(gsum, coarse_inverse, precision=hi)
     beta = lax.all_gather(beta_part, "clus", axis=1, tiled=True)
     back = jnp.dot(beta, one_hot.T, precision=hi)

time: 140 us -> 96.5 us (0.69)
  waiting for transfers between devices: 110 us -> 64.9 us
  other arithmetic: 4.31 us -> 6.21 us
    psum x1 -> x0, waiting for transfers between devices: 110 us -> none  [per_device(): gsum = lax.psum(part_sum, 'wide')]
    all_gather x0 -> x1, waiting for transfers between devices: none -> 64.9 us  [per_device(): terms = lax.all_gather(part_sum, 'wide', axis=0, tiled=False)]
    reduce_sum x0 -> x1, other arithmetic: none -> 1.91 us  [per_device(): gsum = terms.sum(axis=0)]
where the time goes in v1:
time: 96.5 us; the launch traced here: 96.3 us
  waiting for transfers between devices  64.9 us (67%)
  between operations  14.2 us (15%)
  other arithmetic  6.21 us (6%)
  matrix products  4.32 us (4%)
  blocking collectives  3.92 us (4%)
  local copies, waits for them, and re-layouts  2.69 us (3%)
    all_gather x1, waiting for transfers between devices, per_device(): terms = lax.all_gather(part_sum, 'wide', axis=0, tiled=False)  64.9 us
    convert_element_type x1, local copies, waits for them, and re-layouts, per_device(): return (duals.astype(jnp.float32) - delta).astype(jnp.bfloat16)  2.63 us
    another operation x2, other arithmetic, per_device(): lax.linalg.triangular_solve(lower, (forward - back).T, left_side=True, lo...  2.55 us
    all_gather x1, blocking collectives, per_device(): cluster_vec = lax.all_gather(local, 'clus', axis=1, tiled=True)  1.97 us
    all_gather x1, blocking collectives, per_device(): beta = lax.all_gather(beta_part, 'clus', axis=1, tiled=True)  1.95 us
  transfers between devices with their start and end apart: 1, of which 1 were waited for; matrix products, arithmetic and copies ran while one was open for 0% of the time, Pallas kernels for 0%

profile of v1, /device:TPU:0, one launch (start us, length us, event | category | flops | bytes accessed | tf_op | source)
XLA Modules:
  0.0 96.3 jit_solution(3194218232913824929)
XLA Ops:
  6.5 0.0 copy-start
  6.5 0.0 copy-start.2
  6.5 0.0 all-gather.4.cloned.1.call-start
  7.3 0.7 fusion.16
  8.0 1.8 %custom-call.5 = f32[1,24,24]{1,2,0:T(8,128)S(1)} custom-call(f32[1,24,24]{2,1,0:T(8,128)S(1)} %fusion.16), custom_call_target="InvertDiagBlocksLowerTriangular" | custom-call | tf_op jit(solution)/shard_map/triangular_solve | solution.py:32
  9.8 0.8 compare_and_fusion
  10.6 1.0 %broadcast_select_fusion = bf16[2,6,3840]{2,0,1:T(2,128)(2,1)S(1)} fusion(bf16[2,6,3840]{2,0,1:T(2,128)(2,1)} %param.8, pred[2,3840]{1,0:T(4,128)(4,1)S(1)} %compare_and_fusion), kind=kLoop, calls=%fused_computation.7 | loop fusion | flops 46080 | bytes 192000 | tf_op jit(solution)/shard_map/jit(_where)/select_n | solution.py:14
  11.6 1.9 %fusion.4 = f32[96,2,6]{0,2,1:T(8,128)S(1)} fusion(bf16[96,2,3840]{2,1,0:T(2,128)(2,1)} %param.7, bf16[2,6,3840]{2,0,1:T(2,128)(2,1)S(1)} %broadcast_select_fusion), kind=kOutput, calls=%fused_computation.6 | convolution fusion | flops 8847360 | bytes 1571328 | tf_op jit(solution)/shard_map/rsi,ski->rsk/dot_general | solution.py:15
  13.4 2.0 %all-gather.1 = f32[2,12,96]{2,1,0:T(8,128)S(1)} all-gather(f32[1,12,96]{2,1,0:T(8,128)S(1)} %bitcast.36), channel_id=1, replica_groups=mesh['wide'=16,'clus'=2] {'clus'}, dimensions={0}, use_global_device_ids=true | all-gather | bytes 13824 | tf_op jit(solution)/shard_map/all_gather | solution.py:17
  15.4 0.2 fusion.14
  15.6 0.0 copy-done.2
  15.6 0.9 fusion.9
  16.5 0.0 all-gather.4.cloned.1.call-update
  16.6 64.9 %all-gather.4.cloned.1.call-done = f32[1536,384]{1,0:T(8,128)} async-done(((f32[96,384]{1,0:T(8,128)}), f32[1536,384]{1,0:T(8,128)}) %all-gather.4.cloned.1.call-update) | async-done | bytes 2359312 | tf_op jit(solution)/shard_map/all_gather | solution.py:27
  81.5 0.0 copy-start.1
  81.5 1.9 %reduce_sum.9 = f32[96,384]{1,0:T(8,128)S(1)} reduce(f32[16,96,384]{2,1,0:T(8,128)} %bitcast.35, f32[]{:T(128)} %constant.19.clone.1), dimensions={0}, to_apply=%region_0.1 | reduce | flops 552960 | bytes 2506756 | tf_op jit(solution)/shard_map/reduce_sum | solution.py:28
  83.4 0.0 copy-done
  83.4 0.4 fusion.18
  83.8 1.9 %all_gather.15 = f32[96,384]{0,1:T(8,128)S(1)} all-gather(f32[96,192]{0,1:T(8,128)S(1)} %fusion.18), channel_id=1, replica_groups=mesh['wide'=16,'clus'=2] {'clus'}, dimensions={1}, use_global_device_ids=true | all-gather | bytes 221184 | tf_op jit(solution)/shard_map/all_gather | solution.py:30
  85.8 0.2 convolution_subtract_fusion
  86.0 0.1 fusion.12
  86.2 0.0 copy-done.1
  86.2 0.6 fusion.1
  86.8 2.6 %copy.23 = bf16[96,2,3840]{2,1,0:T(2,128)(2,1)} copy(bf16[96,2,3840]{2,0,1:T(8,128)(2,1)S(1)} %fusion.1) | data formatting | bytes 2949120 | tf_op jit(solution)/shard_map/convert_element_type | solution.py:40
  (5 shorter events, 0.1 us)
Async XLA Ops:
  6.5 76.9 %copy-start = (f32[384,192]{0,1:T(8,128)S(1)}, f32[384,192]{0,1:T(8,128)}, u32[]{:S(2)}) copy-start(f32[384,192]{0,1:T(8,128)} %param.13) | copy-start | bytes 884740
  6.5 9.1 %copy-start.2 = (s32[1,24]{1,0:T(1,128)S(1)}, s32[1,24]{1,0:T(1,128)}, u32[]{:S(2)}) copy-start(s32[1,24]{1,0:T(1,128)} %param.12) | copy-start | bytes 292
  6.5 75.0 %all-gather.4.cloned.1.call-start = ((), (), s32[]{:S(2)}) async-start(), calls=%async_computation | async-start | bytes 2506752 | tf_op jit(solution)/shard_map/all_gather | solution.py:27
  81.5 4.7 %copy-start.1 = (bf16[96,2,3840]{2,1,0:T(2,128)(2,1)S(1)}, bf16[96,2,3840]{2,1,0:T(2,128)(2,1)}, u32[]{:S(2)}) copy-start(bf16[96,2,3840]{2,1,0:T(2,128)(2,1)} %param.7) | copy-start | bytes 4423684
Sparse Core Ops, SparseCore 0:
  16.7 64.7 all-gather.3
